TPU v7x, 32 devices: a whole 2x2x4 slice. The times are simulated.
32 devices in a mesh: nest: 2 (over core), rows: 8 (over z, x), sub: 2 (over y).
Axes of the slice: x: 2, y: 2, z: 4, core: 2. Of those that a mesh axis runs over, the one named last changes fastest.
Arguments:
- elevation: float32 [2, 1024, 1024], P('nest', ('rows', 'sub')), may hold values from -6 to 6
- momentum_x: float32 [2, 1024, 1024], P('nest', ('rows', 'sub')), may hold values from -6 to 6
- momentum_y: float32 [2, 1024, 1024], P('nest', ('rows', 'sub')), may hold values from -6 to 6
- depth: float32 [2, 1024, 1024], P('nest', ('rows', 'sub')), may hold values from 0.2 to 1
- wet_mask: int32 [2, 1024, 1024], P('nest', ('rows', 'sub')), may hold values 0 or 1
- inverse_x: float32 [2, 8, 128, 128], P('nest'), may hold values from -1 to 2, as said below
- inverse_y: float32 [2, 8, 128, 128], P('nest'), may hold values from -1 to 2, as said below
- nest_map: int32 [2, 2, 1024], replicated, may hold values from 0 to 1023, as said below
Outputs:
- elevation_out: float32 [2, 1024, 1024], P('nest', ('rows', 'sub'))
- momentum_x_out: float32 [2, 1024, 1024], P('nest', ('rows', 'sub'))
- momentum_y_out: float32 [2, 1024, 1024], P('nest', ('rows', 'sub'))
Inputs may be any that keep to these rules, and one draw needn't show every extreme that they name: nest_map[b, 0, j] is the regional row and nest_map[b, 1, j] the regional column for cell j of the near-field's first (b = 0) or last (b = 1) row; the first row is driven by regional row 0 and the last by regional row 1023, and the column is c0 + j // 2 for one offset c0 shared by both rows, with every column below 1024. `inverse_x`: dense blocks, one for each line block of a section. `inverse_y`: dense blocks, one for each line block of a section.
All inputs are finite; a program needn't handle non-finite values. No bound on the sum of `wet_mask` on one device may be relied on, other than what follows from the above.
Results may differ from a plain program's by a relative error of at most 0.00013.
Values sent between devices are 32-bit elements; how exact they have to be, the bound alone decides.
No kernel may reach another device: no remote copies, remote signals or barrier semaphores. Data moves between devices by JAX's collectives and lax.ppermute only.
A program may use at most 64 MiB of HBM per device.

v0:
```python
import jax
import jax.numpy as jnp
from jax import lax
from jax.sharding import PartitionSpec as P

STEPS = 2
step_ratio = 0.5
dispersion = 0.5
nest_blend = 0.5


def from_behind(value, axis, steps):
    count = lax.axis_size(axis)
    leading, last = (max(0, -steps), min(count, count - steps))
    return lax.ppermute(value, axis, [(source, source + steps) for source in range(leading, last)])


def redistribute(blocks):
    return lax.all_to_all(blocks, ("rows", "sub"), split_axis=0, concat_axis=0, tiled=True)


def to_lines(field):
    rows_here, width = field.shape
    count = lax.axis_size(("rows", "sub"))
    blocks = field.reshape(rows_here, count, width // count).transpose(1, 0, 2)
    moved = redistribute(blocks)
    return moved.reshape(count * rows_here, width // count).T


def from_lines(lines):
    line_width, total_rows = lines.shape
    count = lax.axis_size(("rows", "sub"))
    rows_here = total_rows // count
    blocks = lines.T.reshape(count, rows_here, line_width)
    moved = redistribute(blocks)
    return moved.transpose(1, 0, 2).reshape(rows_here, count * line_width)


def operate_last(field, coef):
    right = jnp.pad(field[:, 1:], ((0, 0), (0, 1)))
    left = jnp.pad(field[:, :-1], ((0, 0), (1, 0)))
    coef_left = jnp.pad(coef[:, :-1], ((0, 0), (1, 0)))
    return field + coef * (field - right) + coef_left * (field - left)


def apply_blocks(field, tables):
    leading, length = field.shape
    group = tables.shape[-1]
    split = field.reshape(leading, length // group, group)
    result = jnp.einsum(
        "kij,rkj->rki",
        tables,
        split,
        precision=lax.Precision.HIGHEST,
        preferred_element_type=jnp.float32,
    )
    return result.reshape(leading, length)


def on_device(elevation, momentum_x, momentum_y, depth, wet_mask, inverse_x, inverse_y, nest_map):
    height = elevation[0]
    flow_x = momentum_x[0]
    flow_y = momentum_y[0]
    depth_here = depth[0]
    wetness = wet_mask[0].astype(jnp.float32)
    rows_here, width = height.shape
    total_rows = lax.axis_size(("rows", "sub")) * rows_here
    tables_x = inverse_x[0]
    tables_y = inverse_y[0]
    start = lax.axis_index(("rows", "sub")) * rows_here
    regional = lax.axis_index("nest") == 0
    nearfield = lax.axis_index("nest") == 1
    global_rows = start + lax.iota(jnp.int32, rows_here)
    top_row = jnp.logical_and(nearfield, global_rows == 0)[:, None]
    bottom_row = jnp.logical_and(nearfield, global_rows == total_rows - 1)[:, None]
    face_x = wetness[:, :-1] * wetness[:, 1:] * (0.5 * (depth_here[:, :-1] + depth_here[:, 1:]))
    face_x = jnp.pad(face_x, ((0, 0), (0, 1)))
    coef_x = dispersion * face_x * face_x
    face_y = jnp.zeros_like(height)
    coef_y = jnp.zeros_like(height)
    coef_lines = jnp.zeros_like(height)
    for step in range(STEPS):
        below = from_behind(jnp.stack([height[0], depth_here[0], wetness[0]]), ("rows", "sub"), -1)
        if step == 0:
            depth_next = jnp.concatenate([depth_here[1:], below[1:2]], 0)
            wet_next = jnp.concatenate([wetness[1:], below[2:3]], 0)
            face_y = wetness * wet_next * (0.5 * (depth_here + depth_next))
            coef_y = dispersion * face_y * face_y
            coef_lines = to_lines(coef_y)
        south = jnp.concatenate([height[1:], below[0:1]], 0)
        east = jnp.pad(height[:, 1:], ((0, 0), (0, 1)))
        push_x = flow_x + step_ratio * face_x * (east - height)
        push_y = flow_y + step_ratio * face_y * (south - height)
        first_x = apply_blocks(push_x, tables_x)
        flow_x = first_x + apply_blocks(push_x - operate_last(first_x, coef_x), tables_x)
        lines = to_lines(push_y)
        first_y = apply_blocks(lines, tables_y)
        flow_y = from_lines(
            first_y + apply_blocks(lines - operate_last(first_y, coef_lines), tables_y)
        )
        flux_x = face_x * flow_x
        flux_y = face_y * flow_y
        west = jnp.pad(flux_x[:, :-1], ((0, 0), (1, 0)))
        above = from_behind(flux_y[-1:], ("rows", "sub"), 1)
        north = jnp.concatenate([above, flux_y[:-1]], 0)
        height = height + step_ratio * (flux_x - west + flux_y - north)
        local_rows = nest_map[:, 0, :] - start
        owned = jnp.logical_and(jnp.logical_and(local_rows >= 0, local_rows < rows_here), regional)
        picked = height[jnp.clip(local_rows, 0, rows_here - 1), nest_map[:, 1, :]]
        packet = lax.psum(jnp.where(owned, picked, 0.0), ("nest", "rows", "sub"))
        blended_top = nest_blend * height + (1.0 - nest_blend) * packet[0][None, :]
        blended_bottom = nest_blend * height + (1.0 - nest_blend) * packet[1][None, :]
        height = jnp.where(top_row, blended_top, jnp.where(bottom_row, blended_bottom, height))
    return (height[None], flow_x[None], flow_y[None])


def solution(mesh):
    in_specs = (
        P("nest", ("rows", "sub"), None),
        P("nest", ("rows", "sub"), None),
        P("nest", ("rows", "sub"), None),
        P("nest", ("rows", "sub"), None),
        P("nest", ("rows", "sub"), None),
        P("nest", None, None, None),
        P("nest", None, None, None),
        P(),
    )
    out_specs = (
        P("nest", ("rows", "sub"), None),
        P("nest", ("rows", "sub"), None),
        P("nest", ("rows", "sub"), None),
    )
    return jax.shard_map(
        on_device, mesh=mesh, in_specs=in_specs, out_specs=out_specs, check_vma=False
    )
```

profile of v0, /device:TPU:0, one launch (start us, length us, event | category | flops | bytes accessed | tf_op | source)
XLA Modules:
  0.0 247.4 jit_solution(11802230985280122733)
XLA Ops:
  0.7 1.1 convert_bitcast_fusion
  1.8 1.3 collective-permute-start
  3.1 0.9 slice_bitcast_fusion.3
  4.4 0.9 squeeze.34
  5.5 1.0 concatenate.45
  6.5 0.9 concatenate.48
  7.4 0.9 concatenate.51
  8.5 0.8 slice.195
  9.6 1.6 fusion.2
  11.5 1.0 reshape.253
  12.6 9.6 %all-to-all-start = ((f32[16,1,4096]{2,1,0:T(1,128)}), f32[16,1,4096]{2,1,0:T(1,128)S(1)}, u32[]{:S(2)}, u32[]{:S(2)}) async-start(f32[16,1,4096]{2,1,0:T(1,128)} %reshape.253), calls=%async_computation | async-start | bytes 524288 | tf_op jit(solution)/shard_map/all_to_all | solution.py:19
  23.0 1.1 convolution_bitcast_fusion.5
  24.1 0.9 fusion.58
  25.2 1.0 reshape.255
  26.2 5.5 %all-to-all-done = f32[16,1,4096]{2,1,0:T(1,128)S(1)} async-done(((f32[16,1,4096]{2,1,0:T(1,128)}), f32[16,1,4096]{2,1,0:T(1,128)S(1)}, u32[]{:S(2)}, u32[]{:S(2)}) %all-to-all-start) | async-done | bytes 262176 | tf_op jit(solution)/shard_map/all_to_all | solution.py:19
  31.8 4.2 %all-to-all-start.1 = ((f32[16,1,4096]{2,1,0:T(1,128)}), f32[16,1,4096]{2,1,0:T(1,128)}, u32[]{:S(2)}, u32[]{:S(2)}) async-start(f32[16,1,4096]{2,1,0:T(1,128)} %reshape.255), calls=%async_computation.1 | async-start | bytes 524288 | tf_op jit(solution)/shard_map/all_to_all | solution.py:19
  36.5 1.3 reduce.12
  37.8 1.0 reshape.254
  38.8 1.3 copy.88
  40.1 1.1 convolution_bitcast_fusion.3
  41.3 0.8 fusion.59
  42.0 2.4 all-to-all-done.1
  44.4 2.2 reduce.13
  46.7 1.0 reshape.256
  47.7 1.2 copy.89
  48.9 2.2 convolution_bitcast_fusion.2
  51.2 1.0 copy.191
  52.2 2.1 reshape.257
  54.2 4.6 %all-to-all-start.2 = ((f32[16,1,4096]{2,1,0:T(1,128)}), f32[16,1,4096]{2,1,0:T(1,128)S(1)}, u32[]{:S(2)}, u32[]{:S(2)}) async-start(f32[16,1,4096]{2,1,0:T(1,128)} %reshape.257), calls=%async_computation.2 | async-start | bytes 524288 | tf_op jit(solution)/shard_map/all_to_all | solution.py:19
  58.8 2.2 convolution_bitcast_fusion.4
  61.8 5.5 %all-to-all-done.2 = f32[16,1,4096]{2,1,0:T(1,128)S(1)} async-done(((f32[16,1,4096]{2,1,0:T(1,128)}), f32[16,1,4096]{2,1,0:T(1,128)S(1)}, u32[]{:S(2)}, u32[]{:S(2)}) %all-to-all-start.2) | async-done | bytes 262176 | tf_op jit(solution)/shard_map/all_to_all | solution.py:19
  67.3 1.3 reduce.14
  68.5 1.0 reshape.258
  69.6 1.2 copy.90
  70.8 1.3 fusion.53
  72.1 3.4 %collective-permute-start.1 = (f32[1,1024]{1,0:T(1,128)S(1)}, f32[1,1024]{1,0:T(1,128)S(1)}, u32[]{:S(2)}, u32[]{:S(2)}) collective-permute-start(f32[1,1024]{1,0:T(1,128)S(1)} %slice.208), channel_id=1, source_target_pairs={{0,1},{1,2},{2,3},{3,4},{4,5},{5,6},{6,7},{7,8},{8,9},{9,10},{10,1... | collective-permute-start | bytes 12296 | tf_op jit(solution)/shard_map/ppermute | solution.py:15
  75.5 1.3 collective-permute-done.1
  76.9 16.6 %gather_fusion = f32[2048]{0:T(1024)S(1)} fusion(f32[64,1024]{1,0:T(8,128)S(1)} %fusion.41, s32[2048]{0:T(1024)S(1)} %bitcast.265), kind=kCustom, calls=%fused_computation | custom fusion | bytes 32768 | tf_op jit(solution)/shard_map/gather | solution.py:109
  93.6 41.4 %psum.14 = f32[2,1024]{1,0:T(2,128)S(1)} all-reduce(f32[2,1024]{1,0:T(2,128)S(1)} %bitcast_select_fusion.1), channel_id=1, replica_groups=mesh['nest'=2,'rows'=8,'sub'=2] {'nest','rows','sub'}, use_global_device_ids=true, to_apply=%region_0.1 | all-reduce | flops 2048 | bytes 16384 | tf_op jit(solution)/shard_map/psum | solution.py:110
  135.2 1.3 collective-permute-start.2
  136.7 4.4 %collective-permute-done.2 = f32[3,1024]{1,0:T(4,128)S(1)} collective-permute-done((f32[3,1024]{1,0:T(4,128)S(1)}, f32[3,1024]{1,0:T(4,128)S(1)}, u32[]{:S(2)}, u32[]{:S(2)}) %collective-permute-start.2) | collective-permute-done | bytes 12320 | tf_op jit(solution)/shard_map/ppermute | solution.py:15
  141.2 1.0 fusion.16
  142.1 2.0 copy.91
  144.2 2.1 reshape.259
  146.2 5.7 %all-to-all-start.3 = ((f32[16,1,4096]{2,1,0:T(1,128)}), f32[16,1,4096]{2,1,0:T(1,128)S(1)}, u32[]{:S(2)}, u32[]{:S(2)}) async-start(f32[16,1,4096]{2,1,0:T(1,128)} %reshape.259), calls=%async_computation.3 | async-start | bytes 524288 | tf_op jit(solution)/shard_map/all_to_all | solution.py:19
  151.9 1.1 fusion.11
  153.1 7.3 %all-to-all-done.3 = f32[16,1,4096]{2,1,0:T(1,128)S(1)} async-done(((f32[16,1,4096]{2,1,0:T(1,128)}), f32[16,1,4096]{2,1,0:T(1,128)S(1)}, u32[]{:S(2)}, u32[]{:S(2)}) %all-to-all-start.3) | async-done | bytes 262176 | tf_op jit(solution)/shard_map/all_to_all | solution.py:19
  160.4 1.3 reduce.15
  161.6 1.0 reshape.260
  162.6 2.1 copy.79
  164.8 1.2 reshape.217
  166.0 1.1 convolution_bitcast_fusion.1
  167.3 1.2 convolution_bitcast_fusion
  168.8 1.0 reshape.261
  169.8 3.5 %all-to-all-start.4 = ((f32[16,1,4096]{2,1,0:T(1,128)}), f32[16,1,4096]{2,1,0:T(1,128)S(1)}, u32[]{:S(2)}, u32[]{:S(2)}) async-start(f32[16,1,4096]{2,1,0:T(1,128)} %reshape.261), calls=%async_computation.4 | async-start | bytes 524288 | tf_op jit(solution)/shard_map/all_to_all | solution.py:19
  173.5 0.8 copy-done.5
  174.3 1.9 bitcast_add_fusion.4
  176.2 5.6 %all-to-all-done.4 = f32[16,1,4096]{2,1,0:T(1,128)S(1)} async-done(((f32[16,1,4096]{2,1,0:T(1,128)}), f32[16,1,4096]{2,1,0:T(1,128)S(1)}, u32[]{:S(2)}, u32[]{:S(2)}) %all-to-all-start.4) | async-done | bytes 262176 | tf_op jit(solution)/shard_map/all_to_all | solution.py:19
  181.9 1.3 reduce.16
  183.6 3.5 %collective-permute-start.3 = (f32[1,1024]{1,0:T(1,128)S(1)}, f32[1,1024]{1,0:T(1,128)S(1)}, u32[]{:S(2)}, u32[]{:S(2)}) collective-permute-start(f32[1,1024]{1,0:T(1,128)S(1)} %slice.221), channel_id=1, source_target_pairs={{0,1},{1,2},{2,3},{3,4},{4,5},{5,6},{6,7},{7,8},{8,9},{9,10},{10,1... | collective-permute-start | bytes 12296 | tf_op jit(solution)/shard_map/ppermute | solution.py:15
  188.1 0.9 copy.93
  189.2 16.6 %gather_fusion.1 = f32[2048]{0:T(1024)S(1)} fusion(f32[64,1024]{1,0:T(8,128)S(1)} %fusion.45, s32[2048]{0:T(1024)S(1)} %bitcast.266), kind=kCustom, calls=%fused_computation.1 | custom fusion | bytes 32768 | tf_op jit(solution)/shard_map/gather | solution.py:109
  205.9 40.7 %psum.15 = f32[2,1024]{1,0:T(2,128)S(1)} all-reduce(f32[2,1024]{1,0:T(2,128)S(1)} %bitcast_select_fusion), channel_id=1, replica_groups=mesh['nest'=2,'rows'=8,'sub'=2] {'nest','rows','sub'}, use_global_device_ids=true, to_apply=%region_1.2 | all-reduce | flops 2048 | bytes 16384 | tf_op jit(solution)/shard_map/psum | solution.py:110
  246.5 0.9 select_bitcast_fusion
  (85 shorter events, 6.6 us)
Async XLA Ops:
  0.6 22.3 %copy-start = (f32[1,8,128,128]{3,2,1,0:T(8,128)S(1)}, f32[1,8,128,128]{3,2,1,0:T(8,128)}, u32[]{:S(2)}) copy-start(f32[1,8,128,128]{3,2,1,0:T(8,128)} %param.13) | copy-start | bytes 1572868
  0.6 1.1 copy-start.3
  0.7 1.2 copy-start.2
  1.8 7.5 %collective-permute-start = (f32[3,1024]{1,0:T(4,128)S(1)}, f32[3,1024]{1,0:T(4,128)S(1)}, u32[]{:S(2)}, u32[]{:S(2)}) collective-permute-start(f32[3,1024]{1,0:T(4,128)S(1)} %pad_maximum_fusion.1), channel_id=1, source_target_pairs={{1,0},{2,1},{3,2},{4,3},{5,4},{6,5},{7,6},{8,7},{9,8},{10,9},{11,1... | collective-permute-start | bytes 36872 | tf_op jit(solution)/shard_map/ppermute | solution.py:15
  7.4 0.9 copy-start.12
  9.6 1.6 copy-start.9
  12.6 9.6 %copy-start.11 = (f32[64,1023]{1,0:T(8,128)S(1)}, f32[64,1023]{1,0:T(8,128)}, u32[]{:S(2)}) copy-start(f32[64,1023]{1,0:T(8,128)} %slice.195) | copy-start | bytes 785668
  12.6 9.6 %copy-start.13 = (f32[1,64,1024]{2,1,0:T(8,128)S(1)}, f32[1,64,1024]{2,1,0:T(8,128)}, u32[]{:S(2)}) copy-start(f32[1,64,1024]{2,1,0:T(8,128)} %param.9) | copy-start | bytes 786436
  12.6 19.2 %all-to-all-start = ((f32[16,1,4096]{2,1,0:T(1,128)}), f32[16,1,4096]{2,1,0:T(1,128)S(1)}, u32[]{:S(2)}, u32[]{:S(2)}) async-start(f32[16,1,4096]{2,1,0:T(1,128)} %reshape.253), calls=%async_computation | async-start | bytes 524288 | tf_op jit(solution)/shard_map/all_to_all | solution.py:19
  22.3 0.7 copy-start.6
  26.2 9.7 %copy-start.14 = (s32[2,2,1024]{2,1,0:T(2,128)S(1)}, s32[2,2,1024]{2,1,0:T(2,128)}, u32[]{:S(2)}) copy-start(s32[2,2,1024]{2,1,0:T(2,128)} %param.15) | copy-start | bytes 49156
  31.8 12.7 %all-to-all-start.1 = ((f32[16,1,4096]{2,1,0:T(1,128)}), f32[16,1,4096]{2,1,0:T(1,128)}, u32[]{:S(2)}, u32[]{:S(2)}) async-start(f32[16,1,4096]{2,1,0:T(1,128)} %reshape.255), calls=%async_computation.1 | async-start | bytes 524288 | tf_op jit(solution)/shard_map/all_to_all | solution.py:19
  38.8 1.3 copy-start.1
  54.2 4.6 %copy-start.7 = (f32[64,1024]{1,0:T(8,128)S(1)}, f32[64,1024]{1,0:T(8,128)}, u32[]{:S(2)}) copy-start(f32[64,1024]{1,0:T(8,128)} %copy-done.6) | copy-start | bytes 786436
  54.2 13.0 %all-to-all-start.2 = ((f32[16,1,4096]{2,1,0:T(1,128)}), f32[16,1,4096]{2,1,0:T(1,128)S(1)}, u32[]{:S(2)}, u32[]{:S(2)}) async-start(f32[16,1,4096]{2,1,0:T(1,128)} %reshape.257), calls=%async_computation.2 | async-start | bytes 524288 | tf_op jit(solution)/shard_map/all_to_all | solution.py:19
  70.8 6.0 %copy-start.8 = (f32[64,1024]{1,0:T(8,128)S(1)}, f32[64,1024]{1,0:T(8,128)}, u32[]{:S(2)}) copy-start(f32[64,1024]{1,0:T(8,128)} %pad_multiply_fusion) | copy-start | bytes 786436
  72.1 4.7 %collective-permute-start.1 = (f32[1,1024]{1,0:T(1,128)S(1)}, f32[1,1024]{1,0:T(1,128)S(1)}, u32[]{:S(2)}, u32[]{:S(2)}) collective-permute-start(f32[1,1024]{1,0:T(1,128)S(1)} %slice.208), channel_id=1, source_target_pairs={{0,1},{1,2},{2,3},{3,4},{4,5},{5,6},{6,7},{7,8},{8,9},{9,10},{10,1... | collective-permute-start | bytes 12296 | tf_op jit(solution)/shard_map/ppermute | solution.py:15
  135.2 5.9 %collective-permute-start.2 = (f32[3,1024]{1,0:T(4,128)S(1)}, f32[3,1024]{1,0:T(4,128)S(1)}, u32[]{:S(2)}, u32[]{:S(2)}) collective-permute-start(f32[3,1024]{1,0:T(4,128)S(1)} %pad_maximum_fusion), channel_id=1, source_target_pairs={{1,0},{2,1},{3,2},{4,3},{5,4},{6,5},{7,6},{8,7},{9,8},{10,9},{11,1... | collective-permute-start | bytes 36872 | tf_op jit(solution)/shard_map/ppermute | solution.py:15
  142.1 9.8 %copy-start.4 = (f32[64,1024]{1,0:T(8,128)}, f32[64,1024]{1,0:T(8,128)S(1)}, u32[]{:S(2)}) copy-start(f32[64,1024]{1,0:T(8,128)S(1)} %get-tuple-element.12) | copy-start | bytes 786436
  146.2 14.1 %all-to-all-start.3 = ((f32[16,1,4096]{2,1,0:T(1,128)}), f32[16,1,4096]{2,1,0:T(1,128)S(1)}, u32[]{:S(2)}, u32[]{:S(2)}) async-start(f32[16,1,4096]{2,1,0:T(1,128)} %reshape.259), calls=%async_computation.3 | async-start | bytes 524288 | tf_op jit(solution)/shard_map/all_to_all | solution.py:19
  169.8 12.0 %all-to-all-start.4 = ((f32[16,1,4096]{2,1,0:T(1,128)}), f32[16,1,4096]{2,1,0:T(1,128)S(1)}, u32[]{:S(2)}, u32[]{:S(2)}) async-start(f32[16,1,4096]{2,1,0:T(1,128)} %reshape.261), calls=%async_computation.4 | async-start | bytes 524288 | tf_op jit(solution)/shard_map/all_to_all | solution.py:19
  173.4 1.0 copy-start.5
  183.5 3.6 %copy-start.10 = (f32[8,64,128]{2,1,0:T(8,128)S(1)}, f32[8,64,128]{2,1,0:T(8,128)}, u32[]{:S(2)}) copy-start(f32[8,64,128]{2,1,0:T(8,128)} %get-tuple-element.35) | copy-start | bytes 786436
  183.6 5.4 %collective-permute-start.3 = (f32[1,1024]{1,0:T(1,128)S(1)}, f32[1,1024]{1,0:T(1,128)S(1)}, u32[]{:S(2)}, u32[]{:S(2)}) collective-permute-start(f32[1,1024]{1,0:T(1,128)S(1)} %slice.221), channel_id=1, source_target_pairs={{0,1},{1,2},{2,3},{3,4},{4,5},{5,6},{6,7},{7,8},{8,9},{9,10},{10,1... | collective-permute-start | bytes 12296 | tf_op jit(solution)/shard_map/ppermute | solution.py:15
where the time goes:
time: 249 us; the launch traced here: 247 us
  blocking collectives  82.1 us (33%)
  local copies, waits for them, and re-layouts  68.1 us (27%)
  starting transfers between devices  37 us (15%)
  waiting for transfers between devices  32.1 us (13%)
  other arithmetic  15.1 us (6%)
  matrix products  11.9 us (5%)
    psum x2, blocking collectives, on_device(): packet = lax.psum(jnp.where(owned, picked, 0.0), ('nest', 'rows', 'sub'))  82.1 us
    gather x4, local copies, waits for them, and re-layouts, on_device(): picked = height[jnp.clip(local_rows, 0, rows_here - 1), nest_map[:, 1, :]]  33.3 us
    all_to_all x5, starting transfers between devices, redistribute(): lax.all_to_all(blocks, ('rows', 'sub'), split_axis=0, concat_axis=0, tile...  27.5 us
    all_to_all x5, waiting for transfers between devices, redistribute(): lax.all_to_all(blocks, ('rows', 'sub'), split_axis=0, concat_axis=0, tile...  26.3 us
    unnamed x40, local copies, waits for them, and re-layouts  13.1 us
    dot_general x8, matrix products, apply_blocks(): jnp.einsum('kij,rkj->rki', tables, split, precision=lax.Precision.HIGHEST...  11.9 us
    ppermute x4, starting transfers between devices, from_behind(): lax.ppermute(value, axis, [(source, source + steps) for source in range(l...  9.45 us
    all_to_all x5, other arithmetic, redistribute(): lax.all_to_all(blocks, ('rows', 'sub'), split_axis=0, concat_axis=0, tile...  7.24 us
  transfers between devices with their start and end apart: 9, of which 7 were waited for; matrix products, arithmetic and copies ran while one was open for 10% of the time, Pallas kernels for 0%

commit v1 on v0

--- a/solution.py
+++ b/solution.py
@@ -107,7 +107,9 @@
         local_rows = nest_map[:, 0, :] - start
         owned = jnp.logical_and(jnp.logical_and(local_rows >= 0, local_rows < rows_here), regional)
         picked = height[jnp.clip(local_rows, 0, rows_here - 1), nest_map[:, 1, :]]
-        packet = lax.psum(jnp.where(owned, picked, 0.0), ("nest", "rows", "sub"))
+        packet = jnp.sum(
+            lax.all_gather(jnp.where(owned, picked, 0.0), ("nest", "rows", "sub")), axis=0
+        )
         blended_top = nest_blend * height + (1.0 - nest_blend) * packet[0][None, :]
         blended_bottom = nest_blend * height + (1.0 - nest_blend) * packet[1][None, :]
         height = jnp.where(top_row, blended_top, jnp.where(bottom_row, blended_bottom, height))

time: 249 us -> 301 us (1.21)
  blocking collectives: 82.1 us -> 134 us
  local copies, waits for them, and re-layouts: 68.1 us -> 64.9 us
    all_gather x0 -> x2, blocking collectives: none -> 134 us  [on_device(): lax.all_gather(jnp.where(owned, picked, 0.0), ('nest', 'rows', 'sub'))]
    psum x2 -> x0, blocking collectives: 82.1 us -> none  [on_device(): packet = lax.psum(jnp.where(owned, picked, 0.0), ('nest', 'rows', 'sub'))]
    unnamed x40 -> x39, local copies, waits for them, and re-layouts: 13.1 us -> 10.6 us
  transfers between devices with their start and end apart: 9 -> 9, of which waited for: 7 -> 7; matrix products, arithmetic and copies ran while one was open for 10% -> 8% of each run, Pallas kernels for 0% -> 0%
where the time goes in v1:
time: 301 us; the launch traced here: 298 us
  blocking collectives  134 us (45%)
  local copies, waits for them, and re-layouts  64.9 us (22%)
  starting transfers between devices  35.2 us (12%)
  waiting for transfers between devices  33.6 us (11%)
  other arithmetic  17.9 us (6%)
  matrix products  12 us (4%)
    all_gather x2, blocking collectives, on_device(): lax.all_gather(jnp.where(owned, picked, 0.0), ('nest', 'rows', 'sub'))  134 us
    gather x4, local copies, waits for them, and re-layouts, on_device(): picked = height[jnp.clip(local_rows, 0, rows_here - 1), nest_map[:, 1, :]]  33.3 us
    all_to_all x5, waiting for transfers between devices, redistribute(): lax.all_to_all(blocks, ('rows', 'sub'), split_axis=0, concat_axis=0, tile...  28.2 us
    all_to_all x5, starting transfers between devices, redistribute(): lax.all_to_all(blocks, ('rows', 'sub'), split_axis=0, concat_axis=0, tile...  26.4 us
    dot_general x8, matrix products, apply_blocks(): jnp.einsum('kij,rkj->rki', tables, split, precision=lax.Precision.HIGHEST...  12 us
    unnamed x39, local copies, waits for them, and re-layouts  10.6 us
    ppermute x4, starting transfers between devices, from_behind(): lax.ppermute(value, axis, [(source, source + steps) for source in range(l...  8.75 us
    all_to_all x5, other arithmetic, redistribute(): lax.all_to_all(blocks, ('rows', 'sub'), split_axis=0, concat_axis=0, tile...  8.21 us
  transfers between devices with their start and end apart: 9, of which 7 were waited for; matrix products, arithmetic and copies ran while one was open for 8% of the time, Pallas kernels for 0%

profile of v1, /device:TPU:0, one launch (start us, length us, event | category | flops | bytes accessed | tf_op | source)
XLA Modules:
  0.0 298.4 jit_solution(8183487731271727504)
XLA Ops:
  0.7 1.1 convert_bitcast_fusion
  1.8 1.3 collective-permute-start
  3.1 0.9 slice_bitcast_fusion.3
  4.3 1.0 squeeze.34
  5.5 1.0 concatenate.45
  6.4 0.9 concatenate.48
  7.4 0.9 concatenate.51
  8.5 0.8 slice.195
  9.6 1.6 fusion.2
  11.5 1.0 reshape.295
  12.5 9.6 %all-to-all-start = ((f32[16,1,4096]{2,1,0:T(1,128)}), f32[16,1,4096]{2,1,0:T(1,128)}, u32[]{:S(2)}, u32[]{:S(2)}) async-start(f32[16,1,4096]{2,1,0:T(1,128)} %reshape.295), calls=%async_computation | async-start | bytes 524288 | tf_op jit(solution)/shard_map/all_to_all | solution.py:19
  22.3 1.1 convolution_bitcast_fusion.5
  23.5 0.9 fusion.59
  24.5 1.0 reshape.297
  25.5 6.3 %all-to-all-done = f32[16,1,4096]{2,1,0:T(1,128)} async-done(((f32[16,1,4096]{2,1,0:T(1,128)}), f32[16,1,4096]{2,1,0:T(1,128)}, u32[]{:S(2)}, u32[]{:S(2)}) %all-to-all-start) | async-done | bytes 262176 | tf_op jit(solution)/shard_map/all_to_all | solution.py:19
  31.8 4.2 %all-to-all-start.1 = ((f32[16,1,4096]{2,1,0:T(1,128)}), f32[16,1,4096]{2,1,0:T(1,128)}, u32[]{:S(2)}, u32[]{:S(2)}) async-start(f32[16,1,4096]{2,1,0:T(1,128)} %reshape.297), calls=%async_computation.1 | async-start | bytes 524288 | tf_op jit(solution)/shard_map/all_to_all | solution.py:19
  36.6 2.2 reduce.12
  38.9 1.0 reshape.296
  39.9 1.3 copy.90
  41.2 1.1 convolution_bitcast_fusion.3
  42.4 0.9 fusion.60
  43.2 1.3 all-to-all-done.1
  44.5 2.2 reduce.13
  46.7 1.0 reshape.298
  47.8 1.2 copy.91
  49.0 2.2 convolution_bitcast_fusion.2
  52.0 1.1 reshape.250
  53.1 1.0 copy.209
  54.0 2.1 reshape.299
  56.1 5.5 %all-to-all-start.2 = ((f32[16,1,4096]{2,1,0:T(1,128)}), f32[16,1,4096]{2,1,0:T(1,128)S(1)}, u32[]{:S(2)}, u32[]{:S(2)}) async-start(f32[16,1,4096]{2,1,0:T(1,128)} %reshape.299), calls=%async_computation.2 | async-start | bytes 524288 | tf_op jit(solution)/shard_map/all_to_all | solution.py:19
  61.6 2.2 convolution_bitcast_fusion.4
  64.6 5.4 %all-to-all-done.2 = f32[16,1,4096]{2,1,0:T(1,128)S(1)} async-done(((f32[16,1,4096]{2,1,0:T(1,128)}), f32[16,1,4096]{2,1,0:T(1,128)S(1)}, u32[]{:S(2)}, u32[]{:S(2)}) %all-to-all-start.2) | async-done | bytes 262176 | tf_op jit(solution)/shard_map/all_to_all | solution.py:19
  70.1 1.3 reduce.14
  71.8 1.2 fusion.54
  73.0 3.4 %collective-permute-start.1 = (f32[1,1024]{1,0:T(1,128)S(1)}, f32[1,1024]{1,0:T(1,128)S(1)}, u32[]{:S(2)}, u32[]{:S(2)}) collective-permute-start(f32[1,1024]{1,0:T(1,128)S(1)} %slice.208), channel_id=1, source_target_pairs={{0,1},{1,2},{2,3},{3,4},{4,5},{5,6},{6,7},{7,8},{8,9},{9,10},{10,1... | collective-permute-start | bytes 12296 | tf_op jit(solution)/shard_map/ppermute | solution.py:15
  76.4 1.3 collective-permute-done.1
  77.7 1.2 fusion.41
  78.9 16.6 %gather_fusion = f32[2048]{0:T(1024)S(1)} fusion(f32[64,1024]{1,0:T(8,128)S(1)} %fusion.41, s32[2048]{0:T(1024)S(1)} %bitcast.276), kind=kCustom, calls=%fused_computation | custom fusion | bytes 32768 | tf_op jit(solution)/shard_map/gather | solution.py:109
  95.6 67.2 %all_gather.8 = f32[32,2,1024]{2,1,0:T(2,128)S(1)} all-gather(f32[1,2,1024]{2,1,0:T(2,128)S(1)} %bitcast_select_fusion.1), channel_id=1, replica_groups=mesh['nest'=2,'rows'=8,'sub'=2] {'nest','rows','sub'}, dimensions={0}, use_global_device_ids=true | all-gather | bytes 270336 | tf_op jit(solution)/shard_map/all_gather | solution.py:111
  163.1 1.3 collective-permute-start.2
  164.5 4.2 %collective-permute-done.2 = f32[3,1024]{1,0:T(4,128)S(1)} collective-permute-done((f32[3,1024]{1,0:T(4,128)S(1)}, f32[3,1024]{1,0:T(4,128)S(1)}, u32[]{:S(2)}, u32[]{:S(2)}) %collective-permute-start.2) | collective-permute-done | bytes 12320 | tf_op jit(solution)/shard_map/ppermute | solution.py:15
  168.7 1.0 fusion.16
  169.7 1.2 copy.93
  170.9 1.0 reshape.301
  171.9 3.5 %all-to-all-start.3 = ((f32[16,1,4096]{2,1,0:T(1,128)}), f32[16,1,4096]{2,1,0:T(1,128)S(1)}, u32[]{:S(2)}, u32[]{:S(2)}) async-start(f32[16,1,4096]{2,1,0:T(1,128)} %reshape.301), calls=%async_computation.3 | async-start | bytes 524288 | tf_op jit(solution)/shard_map/all_to_all | solution.py:19
  175.5 1.1 fusion.11
  176.6 8.7 %all-to-all-done.3 = f32[16,1,4096]{2,1,0:T(1,128)S(1)} async-done(((f32[16,1,4096]{2,1,0:T(1,128)}), f32[16,1,4096]{2,1,0:T(1,128)S(1)}, u32[]{:S(2)}, u32[]{:S(2)}) %all-to-all-start.3) | async-done | bytes 262176 | tf_op jit(solution)/shard_map/all_to_all | solution.py:19
  185.4 1.3 reduce.15
  186.6 1.0 reshape.302
  187.6 2.1 copy.81
  189.8 1.2 reshape.257
  191.0 1.1 convolution_bitcast_fusion.1
  192.3 1.2 convolution_bitcast_fusion
  193.8 1.0 reshape.303
  194.9 3.5 %all-to-all-start.4 = ((f32[16,1,4096]{2,1,0:T(1,128)}), f32[16,1,4096]{2,1,0:T(1,128)S(1)}, u32[]{:S(2)}, u32[]{:S(2)}) async-start(f32[16,1,4096]{2,1,0:T(1,128)} %reshape.303), calls=%async_computation.4 | async-start | bytes 524288 | tf_op jit(solution)/shard_map/all_to_all | solution.py:19
  198.5 0.8 copy-done.7
  199.3 1.9 bitcast_add_fusion.4
  201.2 6.4 %all-to-all-done.4 = f32[16,1,4096]{2,1,0:T(1,128)S(1)} async-done(((f32[16,1,4096]{2,1,0:T(1,128)}), f32[16,1,4096]{2,1,0:T(1,128)S(1)}, u32[]{:S(2)}, u32[]{:S(2)}) %all-to-all-start.4) | async-done | bytes 262176 | tf_op jit(solution)/shard_map/all_to_all | solution.py:19
  207.6 1.3 reduce.16
  209.4 2.8 collective-permute-start.3
  213.1 0.9 copy.95
  214.2 16.6 %gather_fusion.1 = f32[2048]{0:T(1024)S(1)} fusion(f32[64,1024]{1,0:T(8,128)S(1)} %fusion.45, s32[2048]{0:T(1024)S(1)} %bitcast.277), kind=kCustom, calls=%fused_computation.1 | custom fusion | bytes 32768 | tf_op jit(solution)/shard_map/gather | solution.py:109
  230.9 66.4 %all_gather.9 = f32[32,2,1024]{2,1,0:T(2,128)S(1)} all-gather(f32[1,2,1024]{2,1,0:T(2,128)S(1)} %bitcast_select_fusion), channel_id=1, replica_groups=mesh['nest'=2,'rows'=8,'sub'=2] {'nest','rows','sub'}, dimensions={0}, use_global_device_ids=true | all-gather | bytes 270336 | tf_op jit(solution)/shard_map/all_gather | solution.py:111
  297.5 0.9 select_bitcast_fusion
  (86 shorter events, 7.0 us)
Async XLA Ops:
  0.6 21.7 %copy-start = (f32[1,8,128,128]{3,2,1,0:T(8,128)S(1)}, f32[1,8,128,128]{3,2,1,0:T(8,128)}, u32[]{:S(2)}) copy-start(f32[1,8,128,128]{3,2,1,0:T(8,128)} %param.13) | copy-start | bytes 1572868
  0.6 1.1 copy-start.3
  0.7 1.2 copy-start.2
  1.8 7.5 %collective-permute-start = (f32[3,1024]{1,0:T(4,128)S(1)}, f32[3,1024]{1,0:T(4,128)S(1)}, u32[]{:S(2)}, u32[]{:S(2)}) collective-permute-start(f32[3,1024]{1,0:T(4,128)S(1)} %pad_maximum_fusion.1), channel_id=1, source_target_pairs={{1,0},{2,1},{3,2},{4,3},{5,4},{6,5},{7,6},{8,7},{9,8},{10,9},{11,1... | collective-permute-start | bytes 36872 | tf_op jit(solution)/shard_map/ppermute | solution.py:15
  7.4 0.9 copy-start.11
  9.6 1.6 copy-start.8
  12.5 9.7 %copy-start.10 = (f32[64,1023]{1,0:T(8,128)S(1)}, f32[64,1023]{1,0:T(8,128)}, u32[]{:S(2)}) copy-start(f32[64,1023]{1,0:T(8,128)} %slice.195) | copy-start | bytes 785668
  12.5 9.7 %copy-start.12 = (f32[1,64,1024]{2,1,0:T(8,128)S(1)}, f32[1,64,1024]{2,1,0:T(8,128)}, u32[]{:S(2)}) copy-start(f32[1,64,1024]{2,1,0:T(8,128)} %param.9) | copy-start | bytes 786436
  12.5 19.3 %all-to-all-start = ((f32[16,1,4096]{2,1,0:T(1,128)}), f32[16,1,4096]{2,1,0:T(1,128)}, u32[]{:S(2)}, u32[]{:S(2)}) async-start(f32[16,1,4096]{2,1,0:T(1,128)} %reshape.295), calls=%async_computation | async-start | bytes 524288 | tf_op jit(solution)/shard_map/all_to_all | solution.py:19
  25.5 10.5 %copy-start.13 = (s32[2,2,1024]{2,1,0:T(2,128)S(1)}, s32[2,2,1024]{2,1,0:T(2,128)}, u32[]{:S(2)}) copy-start(s32[2,2,1024]{2,1,0:T(2,128)} %param.15) | copy-start | bytes 49156
  31.8 12.7 %all-to-all-start.1 = ((f32[16,1,4096]{2,1,0:T(1,128)}), f32[16,1,4096]{2,1,0:T(1,128)}, u32[]{:S(2)}, u32[]{:S(2)}) async-start(f32[16,1,4096]{2,1,0:T(1,128)} %reshape.297), calls=%async_computation.1 | async-start | bytes 524288 | tf_op jit(solution)/shard_map/all_to_all | solution.py:19
  39.9 1.3 copy-start.1
  56.1 14.0 %all-to-all-start.2 = ((f32[16,1,4096]{2,1,0:T(1,128)}), f32[16,1,4096]{2,1,0:T(1,128)S(1)}, u32[]{:S(2)}, u32[]{:S(2)}) async-start(f32[16,1,4096]{2,1,0:T(1,128)} %reshape.299), calls=%async_computation.2 | async-start | bytes 524288 | tf_op jit(solution)/shard_map/all_to_all | solution.py:19
  63.9 0.8 copy-start.4
  73.0 4.7 %collective-permute-start.1 = (f32[1,1024]{1,0:T(1,128)S(1)}, f32[1,1024]{1,0:T(1,128)S(1)}, u32[]{:S(2)}, u32[]{:S(2)}) collective-permute-start(f32[1,1024]{1,0:T(1,128)S(1)} %slice.208), channel_id=1, source_target_pairs={{0,1},{1,2},{2,3},{3,4},{4,5},{5,6},{6,7},{7,8},{8,9},{9,10},{10,1... | collective-permute-start | bytes 12296 | tf_op jit(solution)/shard_map/ppermute | solution.py:15
  163.1 5.6 %collective-permute-start.2 = (f32[3,1024]{1,0:T(4,128)S(1)}, f32[3,1024]{1,0:T(4,128)S(1)}, u32[]{:S(2)}, u32[]{:S(2)}) collective-permute-start(f32[3,1024]{1,0:T(4,128)S(1)} %pad_maximum_fusion), channel_id=1, source_target_pairs={{1,0},{2,1},{3,2},{4,3},{5,4},{6,5},{7,6},{8,7},{9,8},{10,9},{11,1... | collective-permute-start | bytes 36872 | tf_op jit(solution)/shard_map/ppermute | solution.py:15
  164.5 4.2 %copy-start.5 = (f32[8,8,8,128]{3,2,1,0:T(8,128)S(1)}, f32[8,8,8,128]{3,2,1,0:T(8,128)}, u32[]{:S(2)}) copy-start(f32[8,8,8,128]{3,2,1,0:T(8,128)} %copy-done.4) | copy-start | bytes 786436
  169.7 5.8 %copy-start.6 = (f32[64,1024]{1,0:T(8,128)}, f32[64,1024]{1,0:T(8,128)S(1)}, u32[]{:S(2)}) copy-start(f32[64,1024]{1,0:T(8,128)S(1)} %get-tuple-element.12) | copy-start | bytes 786436
  171.9 13.4 %all-to-all-start.3 = ((f32[16,1,4096]{2,1,0:T(1,128)}), f32[16,1,4096]{2,1,0:T(1,128)S(1)}, u32[]{:S(2)}, u32[]{:S(2)}) async-start(f32[16,1,4096]{2,1,0:T(1,128)} %reshape.301), calls=%async_computation.3 | async-start | bytes 524288 | tf_op jit(solution)/shard_map/all_to_all | solution.py:19
  194.9 12.8 %all-to-all-start.4 = ((f32[16,1,4096]{2,1,0:T(1,128)}), f32[16,1,4096]{2,1,0:T(1,128)S(1)}, u32[]{:S(2)}, u32[]{:S(2)}) async-start(f32[16,1,4096]{2,1,0:T(1,128)} %reshape.303), calls=%async_computation.4 | async-start | bytes 524288 | tf_op jit(solution)/shard_map/all_to_all | solution.py:19
  198.4 1.0 copy-start.7
  209.3 2.9 copy-start.9
  209.4 4.7 %collective-permute-start.3 = (f32[1,1024]{1,0:T(1,128)S(1)}, f32[1,1024]{1,0:T(1,128)S(1)}, u32[]{:S(2)}, u32[]{:S(2)}) collective-permute-start(f32[1,1024]{1,0:T(1,128)S(1)} %slice.221), channel_id=1, source_target_pairs={{0,1},{1,2},{2,3},{3,4},{4,5},{5,6},{6,7},{7,8},{8,9},{9,10},{10,1... | collective-permute-start | bytes 12296 | tf_op jit(solution)/shard_map/ppermute | solution.py:15
